TPU v7x, 32 devices: a whole 2x2x4 slice. The times are simulated.
32 devices in a mesh: group: 4 (over z), shard: 8 (over y, x, core).
Axes of the slice: x: 2, y: 2, z: 4, core: 2. Of those that a mesh axis runs over, the one named last changes fastest.
Arguments:
- query_hidden: bfloat16 [32, 32, 768], P(('group', 'shard')), may hold values from -6 to 6
- positive_hidden: bfloat16 [32, 64, 768], P(('group', 'shard')), may hold values from -6 to 6
- passage_store: bfloat16 [256, 64, 768], P('shard'), may hold values from -6 to 6
- negative_ids: int32 [32, 8], P(('group', 'shard')), may hold values from 0 to 255, as said below
- teacher_margins: int32 [32, 8], P(('group', 'shard')), may hold values from -4096 to 4095
- transform_weight: bfloat16 [768, 768], replicated, may hold values from -0.21875 to 0.21875
- vocab_weight: bfloat16 [768, 15360], P(None, 'shard'), may hold values from -0.21875 to 0.21875
- dense_weight: bfloat16 [768, 768], replicated, may hold values from -0.21875 to 0.21875
Outputs:
- student_margin: float32 [32, 8], P(('group', 'shard'))
- dense_grad: float32 [768, 768], replicated
Inputs may be any that keep to these rules, and one draw needn't show every extreme that they name: `negative_ids`: passage p is held by shard index p // 32. Among the 8 negatives of one index of group and shard, every store index is named by none or exactly 2 of them; one store index, drawn from the seed, is named 2 times by every index of group and shard.
All inputs are finite; a program needn't handle non-finite values.
Results may differ from a plain program's by a relative error of at most 0.0029.
Values may be sent and summed in bfloat16 or wider, within the bound.
A program may use at most 128 MiB of HBM per device.

v0:
```python
from functools import partial
import math
import jax
import jax.numpy as jnp
from jax import lax
from jax.sharding import PartitionSpec as P

CAP = 2


def encode(hidden, transform_weight):
    mixed_rows = jnp.dot(hidden, transform_weight, preferred_element_type=jnp.float32)
    active = jax.nn.gelu(mixed_rows, approximate=False)
    centre = jnp.mean(active, axis=-1, keepdims=True)
    spread = jnp.mean(jnp.square(active - centre), axis=-1, keepdims=True)
    return ((active - centre) * lax.rsqrt(spread + 1e-05)).astype(jnp.bfloat16)


def pool_single(sequence, vocab_weight):
    logits = jnp.dot(sequence, vocab_weight, preferred_element_type=jnp.float32)
    return jnp.max(jnp.log1p(jnp.maximum(logits, 0.0)), axis=0)


def pool_sequences(block_rows, offset, vocab_weight):
    return lax.map(partial(pool_single, vocab_weight=vocab_weight), block_rows, batch_size=8)


def add_outer(running, pieces):
    return running + jnp.einsum("rd,re->de", pieces[0], pieces[1], precision=lax.Precision.HIGHEST)


def body(
    query_hidden,
    positive_hidden,
    passage_store,
    negative_ids,
    teacher_margins,
    transform_weight,
    vocab_weight,
    dense_weight,
):
    shards = lax.axis_size("shard")
    queries_dev, negatives = negative_ids.shape
    store_rows, length, width = passage_store.shape
    vocab_total = vocab_weight.shape[1] * shards
    pooler = partial(pool_sequences, vocab_weight=vocab_weight)
    query_coded = encode(query_hidden, transform_weight)
    positive_coded = encode(positive_hidden, transform_weight)
    query_pool = pooler(lax.all_gather(query_coded, "shard", axis=0, tiled=True), jnp.int32(0))
    neg_total = queries_dev * negatives
    flat_ids = negative_ids.reshape(neg_total)
    owner_of = flat_ids // store_rows
    local_row = flat_ids % store_rows
    shard_ids = jnp.arange(shards, dtype=jnp.int32)
    owner_hit = (owner_of[:, None] == shard_ids[None, :]).astype(jnp.int32)
    earlier = jnp.cumsum(owner_hit, axis=0) - owner_hit
    slot_rank = jnp.sum(earlier * owner_hit, axis=1)
    slot_ids = jnp.arange(CAP, dtype=jnp.int32)
    slot_hit = (owner_hit[:, :, None] > 0) & (slot_rank[:, None, None] == slot_ids[None, None, :])
    asked_rows = jnp.sum(jnp.where(slot_hit, local_row[:, None, None], 0), axis=0)
    requests = jnp.where(jnp.any(slot_hit, axis=0), asked_rows, -1)
    asked_for = lax.all_to_all(requests, "shard", split_axis=0, concat_axis=0, tiled=True)
    is_valid = asked_for >= 0
    served = passage_store[jnp.clip(asked_for, 0, store_rows - 1)]
    served = jnp.where(is_valid[:, :, None, None], served, jnp.zeros((), served.dtype))
    fetched = lax.all_to_all(served, "shard", split_axis=0, concat_axis=0, tiled=True)
    negative_hidden = fetched.reshape(shards * CAP, length, width)[owner_of * CAP + slot_rank]
    negative_coded = encode(negative_hidden, transform_weight)
    passages = jnp.concatenate(
        [positive_coded[:, None], negative_coded.reshape(queries_dev, negatives, length, width)],
        axis=1,
    )
    passages = passages.reshape(queries_dev * (1 + negatives), length, width)
    passage_pool = pooler(lax.all_gather(passages, "shard", axis=0, tiled=True), jnp.int32(0))
    passage_pool = passage_pool.reshape(shards * queries_dev, 1 + negatives, -1)
    pair_terms = jnp.einsum("qv,qjv->qj", query_pool, passage_pool, precision=lax.Precision.HIGHEST)
    sparse = lax.psum_scatter(pair_terms, "shard", scatter_dimension=0, tiled=True) / math.sqrt(
        vocab_total
    )
    inv_root = 1.0 / math.sqrt(width)
    query_cls = query_hidden[:, 0, :]
    positive_cls = positive_hidden[:, 0, :]
    negative_cls = negative_hidden[:, 0, :].reshape(queries_dev, negatives, width)
    query_vec = jnp.dot(query_cls, dense_weight, preferred_element_type=jnp.float32)
    positive_vec = jnp.dot(positive_cls, dense_weight, preferred_element_type=jnp.float32)
    negative_vec = jnp.dot(negative_cls, dense_weight, preferred_element_type=jnp.float32)
    dense_pos = jnp.sum(query_vec * positive_vec, axis=1) * inv_root
    dense_neg = (
        jnp.einsum("qd,qkd->qk", query_vec, negative_vec, precision=lax.Precision.HIGHEST)
        * inv_root
    )
    pos_score = sparse[:, 0] + dense_pos
    neg_score = sparse[:, 1:] + dense_neg
    margin = pos_score[:, None] - neg_score
    target = teacher_margins.astype(jnp.float32) / 1024.0
    coef = (margin - target) / negatives
    coef_total = jnp.sum(coef, axis=1)
    grad_query = (
        coef_total[:, None] * positive_vec
        - jnp.einsum("qk,qkd->qd", coef, negative_vec, precision=lax.Precision.HIGHEST)
    ) * inv_root
    grad_positive = coef_total[:, None] * query_vec * inv_root
    grad_negative = -coef[:, :, None] * query_vec[:, None, :] * inv_root
    states = jnp.concatenate(
        [query_cls, positive_cls, negative_cls.reshape(-1, width)], axis=0
    ).astype(jnp.float32)
    factors = jnp.concatenate([grad_query, grad_positive, grad_negative.reshape(-1, width)], axis=0)
    empty = jnp.zeros((width, width), jnp.float32)
    dense_grad = add_outer(
        empty,
        (
            lax.all_gather(states, ("group", "shard"), axis=0, tiled=True),
            lax.all_gather(factors, ("group", "shard"), axis=0, tiled=True),
        ),
    )
    return (margin, dense_grad)


def solution(mesh):
    in_specs = (
        P(("group", "shard"), None, None),
        P(("group", "shard"), None, None),
        P("shard", None, None),
        P(("group", "shard"), None),
        P(("group", "shard"), None),
        P(),
        P(None, "shard"),
        P(),
    )
    out_specs = (P(("group", "shard"), None), P())
    return jax.shard_map(body, mesh=mesh, in_specs=in_specs, out_specs=out_specs, check_vma=False)
```

profile of v0, /device:TPU:0, one launch (start us, length us, event | category | flops | bytes accessed | tf_op | source)
XLA Modules:
  0.0 263.6 jit_solution(15380211158896153419)
XLA Ops:
  8.6 9.7 %all_to_all.11 = s32[8,1,2]{2,1,0:T(1,128)S(1)} all-to-all(s32[8,1,2]{2,1,0:T(1,128)S(1)} %copy.29), channel_id=1, replica_groups=mesh['group'=4,'shard'=8] {'shard'}, dimensions={0} | all-to-all | bytes 128 | tf_op jit(solution)/shard_map/all_to_all | solution.py:62
  20.4 2.7 %broadcast_select_fusion = bf16[8,2,64,768]{3,2,1,0:T(8,128)(2,1)} fusion(bf16[8,2,64,768]{3,2,1,0:T(8,128)(2,1)} %bitcast.160, pred[8,2]{1,0:T(8,128)(4,1)S(1)} %copy.31), kind=kLoop, calls=%fused_computation.37 | loop fusion | flops 786432 | bytes 3145744 | tf_op jit(solution)/shard_map/jit(_where)/select_n | solution.py:65
  23.1 4.4 %all-to-all-start.1 = ((bf16[8,2,64,768]{3,2,1,0:T(8,128)(2,1)}), bf16[8,2,64,768]{3,2,1,0:T(8,128)(2,1)}, u32[]{:S(2)}, u32[]{:S(2)}) async-start(bf16[8,2,64,768]{3,2,1,0:T(8,128)(2,1)} %broadcast_select_fusion), calls=%async_computation.1 | async-start | bytes 3145728 | tf_op jit(solution)/shard_map/all_to_all | solution.py:66
  30.0 18.5 %all-to-all-done.1 = bf16[8,2,64,768]{3,2,1,0:T(8,128)(2,1)} async-done(((bf16[8,2,64,768]{3,2,1,0:T(8,128)(2,1)}), bf16[8,2,64,768]{3,2,1,0:T(8,128)(2,1)}, u32[]{:S(2)}, u32[]{:S(2)}) %all-to-all-start.1) | async-done | bytes 1572896 | tf_op jit(solution)/shard_map/all_to_all | solution.py:66
  48.6 2.9 %gather_fusion.1 = bf16[8,64,768]{2,1,0:T(8,128)(2,1)} fusion(bf16[16,64,768]{2,1,0:T(8,128)(2,1)} %bitcast.14, s32[1024]{0:T(1024)S(1)} %pad_clamp_fusion), kind=kCustom, calls=%fused_computation.1 | custom fusion | bytes 1572896 | tf_op jit(solution)/shard_map/gather | solution.py:67
  51.4 2.8 %fusion.31 = (u8[64,768]{1,0:T(8,128)(4,1)S(1)}, u8[64,768]{1,0:T(8,128)(4,1)S(1)}, u8[64,768]{1,0:T(8,128)(4,1)S(1)}, f32[8,64,768]{2,1,0:T(8,128)S(1)}) fusion(bf16[8,64,768]{2,1,0:T(8,128)(2,1)} %gather_fusion.1, bf16[768,768]{1,0:T(8,128)(2,1)} %param.15), kind=kOutput, calls=%fused_computation.51 | convolution fusion | flops 611696640 | bytes 3686400 | tf_op jit(solution)/shard_map/dot_general | solution.py:12
  54.3 3.8 %fusion.75 = (f32[8,64]{1,0:T(8,128)S(1)}, f32[8,64,768]{2,1,0:T(8,128)S(1)}) fusion(u8[64,768]{1,0:T(8,128)(4,1)S(1)} %get-tuple-element.38, u8[64,768]{1,0:T(8,128)(4,1)S(1)} %get-tuple-element.39, f32[8,64,768]{2,1,0:T(8,128)S(1)} %get-tuple-element.56, u8[64,768]{1,0:T(8,128)(4,1)S(1)} %get-tuple-element.37), kind=kLoop, calls=%fused_computation.154 | loop fusion | flops 28311040 | bytes 3295232 | tf_op jit(solution)/shard_map/reduce_sum | solution.py:14
  67.3 10.4 %all-gather = bf16[256,768]{1,0:T(8,128)(2,1)S(1)} all-gather(bf16[32,768]{1,0:T(8,128)(2,1)S(1)} %multiply_convert_fusion.2), channel_id=2, replica_groups=mesh['group'=4,'shard'=8] {'shard'}, dimensions={0}, use_global_device_ids=true | all-gather | bytes 442368 | tf_op jit(solution)/shard_map/all_gather | solution.py:49
  80.1 50.6 %all-gather.2 = f32[32,10,768]{2,1,0:T(8,128)} all-gather(f32[1,10,768]{2,1,0:T(8,128)S(1)} %fusion.62), channel_id=1, replica_groups=mesh['group'=4,'shard'=8] {'group','shard'}, dimensions={0}, use_global_device_ids=true | all-gather | bytes 1013760 | tf_op jit(solution)/shard_map/all_gather | solution.py:112
  130.8 2.5 reshape.544
  134.8 48.1 %while.2 = (s32[]{:T(128)}, f32[9,8,1920]{2,1,0:T(8,128)}, bf16[9,8,64,768]{3,2,1,0:T(8,128)(2,1)}, bf16[768,1920]{1,0:T(8,128)(2,1)}, s32[]{:T(128)}) while((s32[]{:T(128)}, f32[9,8,1920]{2,1,0:T(8,128)}, bf16[9,8,64,768]{3,2,1,0:T(8,128)(2,1)}, bf16[768,1920]{1,0:T(8,128)(2,1)}, s32[]{:T(128)}) %tuple.40), condition=%wide.region_13.14_spmd, body=%wide.region_11.13_spmd.sunk | while | flops 1511900160 | bytes 3919949 | solution.py:25
  134.8 4.7 %log-plus-one_reduce_fusion.2 = f32[8,1920]{1,0:T(8,128)S(1)} fusion(bf16[768,1920]{1,0:T(8,128)(2,1)} %get-tuple-element.102, bf16[9,8,64,768]{3,2,1,0:T(8,128)(2,1)} %get-tuple-element.101, s32[]{:T(128)S(6)} %copy.45), kind=kOutput, calls=%fused_computation.2.clone.1 | convolution fusion | flops 1511900160 | bytes 3796996 | tf_op jit(solution)/shard_map/while/body/eval_jaxpr/vmap()/dot_general | solution.py:20
  140.2 4.7 %log-plus-one_reduce_fusion.2 = f32[8,1920]{1,0:T(8,128)S(1)} fusion(bf16[768,1920]{1,0:T(8,128)(2,1)} %get-tuple-element.102, bf16[9,8,64,768]{3,2,1,0:T(8,128)(2,1)} %get-tuple-element.101, s32[]{:T(128)S(6)} %copy.45), kind=kOutput, calls=%fused_computation.2.clone.1 | convolution fusion | flops 1511900160 | bytes 3796996 | tf_op jit(solution)/shard_map/while/body/eval_jaxpr/vmap()/dot_general | solution.py:20
  145.5 4.7 %log-plus-one_reduce_fusion.2 = f32[8,1920]{1,0:T(8,128)S(1)} fusion(bf16[768,1920]{1,0:T(8,128)(2,1)} %get-tuple-element.102, bf16[9,8,64,768]{3,2,1,0:T(8,128)(2,1)} %get-tuple-element.101, s32[]{:T(128)S(6)} %copy.45), kind=kOutput, calls=%fused_computation.2.clone.1 | convolution fusion | flops 1511900160 | bytes 3796996 | tf_op jit(solution)/shard_map/while/body/eval_jaxpr/vmap()/dot_general | solution.py:20
  150.9 4.7 %log-plus-one_reduce_fusion.2 = f32[8,1920]{1,0:T(8,128)S(1)} fusion(bf16[768,1920]{1,0:T(8,128)(2,1)} %get-tuple-element.102, bf16[9,8,64,768]{3,2,1,0:T(8,128)(2,1)} %get-tuple-element.101, s32[]{:T(128)S(6)} %copy.45), kind=kOutput, calls=%fused_computation.2.clone.1 | convolution fusion | flops 1511900160 | bytes 3796996 | tf_op jit(solution)/shard_map/while/body/eval_jaxpr/vmap()/dot_general | solution.py:20
  156.2 4.7 %log-plus-one_reduce_fusion.2 = f32[8,1920]{1,0:T(8,128)S(1)} fusion(bf16[768,1920]{1,0:T(8,128)(2,1)} %get-tuple-element.102, bf16[9,8,64,768]{3,2,1,0:T(8,128)(2,1)} %get-tuple-element.101, s32[]{:T(128)S(6)} %copy.45), kind=kOutput, calls=%fused_computation.2.clone.1 | convolution fusion | flops 1511900160 | bytes 3796996 | tf_op jit(solution)/shard_map/while/body/eval_jaxpr/vmap()/dot_general | solution.py:20
  161.6 4.7 %log-plus-one_reduce_fusion.2 = f32[8,1920]{1,0:T(8,128)S(1)} fusion(bf16[768,1920]{1,0:T(8,128)(2,1)} %get-tuple-element.102, bf16[9,8,64,768]{3,2,1,0:T(8,128)(2,1)} %get-tuple-element.101, s32[]{:T(128)S(6)} %copy.45), kind=kOutput, calls=%fused_computation.2.clone.1 | convolution fusion | flops 1511900160 | bytes 3796996 | tf_op jit(solution)/shard_map/while/body/eval_jaxpr/vmap()/dot_general | solution.py:20
  166.9 4.7 %log-plus-one_reduce_fusion.2 = f32[8,1920]{1,0:T(8,128)S(1)} fusion(bf16[768,1920]{1,0:T(8,128)(2,1)} %get-tuple-element.102, bf16[9,8,64,768]{3,2,1,0:T(8,128)(2,1)} %get-tuple-element.101, s32[]{:T(128)S(6)} %copy.45), kind=kOutput, calls=%fused_computation.2.clone.1 | convolution fusion | flops 1511900160 | bytes 3796996 | tf_op jit(solution)/shard_map/while/body/eval_jaxpr/vmap()/dot_general | solution.py:20
  172.3 4.7 %log-plus-one_reduce_fusion.2 = f32[8,1920]{1,0:T(8,128)S(1)} fusion(bf16[768,1920]{1,0:T(8,128)(2,1)} %get-tuple-element.102, bf16[9,8,64,768]{3,2,1,0:T(8,128)(2,1)} %get-tuple-element.101, s32[]{:T(128)S(6)} %copy.45), kind=kOutput, calls=%fused_computation.2.clone.1 | convolution fusion | flops 1511900160 | bytes 3796996 | tf_op jit(solution)/shard_map/while/body/eval_jaxpr/vmap()/dot_general | solution.py:20
  177.6 4.7 %log-plus-one_reduce_fusion.2 = f32[8,1920]{1,0:T(8,128)S(1)} fusion(bf16[768,1920]{1,0:T(8,128)(2,1)} %get-tuple-element.102, bf16[9,8,64,768]{3,2,1,0:T(8,128)(2,1)} %get-tuple-element.101, s32[]{:T(128)S(6)} %copy.45), kind=kOutput, calls=%fused_computation.2.clone.1 | convolution fusion | flops 1511900160 | bytes 3796996 | tf_op jit(solution)/shard_map/while/body/eval_jaxpr/vmap()/dot_general | solution.py:20
  185.0 2.5 fusion.56
  187.5 12.1 %all-reduce = f32[8,9]{1,0:T(8,128)S(1)} all-reduce(f32[8,9]{1,0:T(8,128)S(1)} %bitcast.165), channel_id=4, replica_groups=mesh['group'=4,'shard'=8] {'shard'}, use_global_device_ids=true, to_apply=%region_14.15.clone | all-reduce | flops 72 | bytes 576
  203.4 44.1 %all-gather.3 = f32[32,10,768]{2,1,0:T(8,128)} all-gather(f32[1,10,768]{2,1,0:T(8,128)S(1)} %maximum_bitcast_fusion.1), channel_id=1, replica_groups=mesh['group'=4,'shard'=8] {'group','shard'}, dimensions={0}, use_global_device_ids=true | all-gather | bytes 1013760 | tf_op jit(solution)/shard_map/all_gather | solution.py:113
  249.9 6.9 %fusion.81 = f32[768,768]{1,0:T(8,128)} fusion(f32[320,768]{1,0:T(8,128)} %reshape.544, f32[320,768]{1,0:T(8,128)} %reshape.546), kind=kOutput, calls=%fused_computation.159 | convolution fusion | flops 2264924160 | bytes 4325376 | tf_op jit(solution)/shard_map/rd,re->de/dot_general | solution.py:29
  (84 shorter events, 32.1 us)
Async XLA Ops:
  7.2 11.4 %copy-start = (bf16[32,64,768]{2,1,0:T(8,128)(2,1)S(1)}, bf16[32,64,768]{2,1,0:T(8,128)(2,1)}, u32[]{:S(2)}) copy-start(bf16[32,64,768]{2,1,0:T(8,128)(2,1)} %param.12) | copy-start | bytes 9437188
  23.1 4.5 %copy-start.5 = (s32[1,8]{1,0:T(1,128)S(1)}, s32[1,8]{1,0:T(1,128)}, u32[]{:S(2)}) copy-start(s32[1,8]{1,0:T(1,128)} %param.13) | copy-start | bytes 100
  23.1 4.5 %copy-start.2 = (bf16[1,64,768]{2,1,0:T(8,128)(2,1)S(1)}, bf16[1,64,768]{2,1,0:T(8,128)(2,1)}, u32[]{:S(2)}) copy-start(bf16[1,64,768]{2,1,0:T(8,128)(2,1)} %param.11) | copy-start | bytes 294916
  23.1 25.4 %all-to-all-start.1 = ((bf16[8,2,64,768]{3,2,1,0:T(8,128)(2,1)}), bf16[8,2,64,768]{3,2,1,0:T(8,128)(2,1)}, u32[]{:S(2)}, u32[]{:S(2)}) async-start(bf16[8,2,64,768]{3,2,1,0:T(8,128)(2,1)} %broadcast_select_fusion), calls=%async_computation.1 | async-start | bytes 3145728 | tf_op jit(solution)/shard_map/all_to_all | solution.py:66
  27.6 107.3 %all-gather.6.cloned.1.call-start = ((), (), s32[]{:S(2)}) async-start(), calls=%async_computation.2 | async-start | bytes 7962624 | tf_op jit(solution)/shard_map/all_gather | solution.py:74
  58.7 1.1 copy-start.6
  58.7 3.3 %copy-start.1 = (bf16[1,32,768]{2,1,0:T(8,128)(2,1)S(1)}, bf16[1,32,768]{2,1,0:T(8,128)(2,1)}, u32[]{:S(2)}) copy-start(bf16[1,32,768]{2,1,0:T(8,128)(2,1)} %param.10) | copy-start | bytes 147460
  64.9 12.8 %copy-start.4 = (bf16[768,1920]{1,0:T(8,128)(2,1)S(1)}, bf16[768,1920]{1,0:T(8,128)(2,1)}, u32[]{:S(2)}) copy-start(bf16[768,1920]{1,0:T(8,128)(2,1)} %param.16) | copy-start | bytes 8847364
  182.9 17.4 %copy-start.3 = (s32[1,8]{1,0:T(1,128)S(1)}, s32[1,8]{1,0:T(1,128)}, u32[]{:S(2)}) copy-start(s32[1,8]{1,0:T(1,128)} %param.14) | copy-start | bytes 100
Sparse Core Ops, SparseCore 0:
  59.9 59.8 all-gather.5
where the time goes:
time: 264 us
  blocking collectives  127 us (48%)
  matrix products  66.2 us (25%)
  local copies, waits for them, and re-layouts  19.4 us (7%)
  waiting for transfers between devices  18.6 us (7%)
  between operations  15.1 us (6%)
  other arithmetic  12.9 us (5%)
  starting transfers between devices  4.46 us (2%)
    all_gather x1, blocking collectives, body(): lax.all_gather(states, ('group', 'shard'), axis=0, tiled=True)  50.6 us
    all_gather x1, blocking collectives, body(): lax.all_gather(factors, ('group', 'shard'), axis=0, tiled=True)  44.1 us
    dot_general x10, matrix products, pool_single(): logits = jnp.dot(sequence, vocab_weight, preferred_element_type=jnp.float32)  43.8 us
    all_to_all x1, waiting for transfers between devices, body(): lax.all_to_all(served, 'shard', split_axis=0, concat_axis=0, tiled=True)  18.5 us
    unnamed x1, blocking collectives  12.1 us
    all_gather x1, blocking collectives, body(): lax.all_gather(query_coded, 'shard', axis=0, tiled=True)  10.4 us
    all_to_all x1, blocking collectives, body(): lax.all_to_all(requests, 'shard', split_axis=0, concat_axis=0, tiled=True)  9.68 us
    dot_general x3, matrix products, encode(): jnp.dot(hidden, transform_weight, preferred_element_type=jnp.float32)  6.94 us
  transfers between devices with their start and end apart: 2, of which 1 were waited for; matrix products, arithmetic and copies ran while one was open for 6% of the time, Pallas kernels for 0%

commit v1 on v0

--- a/solution.py
+++ b/solution.py
@@ -6,6 +6,18 @@
 from jax.sharding import PartitionSpec as P
 
 CAP = 2
+
+
+def doubled_up(x, axis, dim):
+    ways, here = (lax.axis_size(axis), lax.axis_index(axis))
+    grown, reach = (x, 1)
+    while reach < ways:
+        theirs = lax.ppermute(grown, axis, [(d, d ^ reach) for d in range(ways)])
+        mine_first = jnp.concatenate([grown, theirs], axis=dim)
+        theirs_first = jnp.concatenate([theirs, grown], axis=dim)
+        grown = jnp.where(here & reach == 0, mine_first, theirs_first)
+        reach = 2 * reach
+    return grown
 
 
 def encode(hidden, transform_weight):
@@ -109,7 +121,7 @@
     dense_grad = add_outer(
         empty,
         (
-            lax.all_gather(states, ("group", "shard"), axis=0, tiled=True),
+            doubled_up(states, ("group", "shard"), 0),
             lax.all_gather(factors, ("group", "shard"), axis=0, tiled=True),
         ),
     )

time: 264 us -> 242 us (0.917)
  blocking collectives: 127 us -> 77.5 us
  waiting for transfers between devices: 18.6 us -> 38.7 us
  starting transfers between devices: 4.46 us -> 13.2 us
    all_gather x1 -> x0, blocking collectives: 50.6 us -> none  [body(): lax.all_gather(states, ('group', 'shard'), axis=0, tiled=True)]
    all_gather x1, waiting for transfers between devices: 0.01 us -> 13 us  [body(): lax.all_gather(passages, 'shard', axis=0, tiled=True)]
    ppermute x0 -> x5, starting transfers between devices: none -> 8.77 us  [doubled_up(): theirs = lax.ppermute(grown, axis, [(d, d ^ reach) for d in range(ways)])]
    ppermute x0 -> x5, waiting for transfers between devices: none -> 7.1 us  [doubled_up(): theirs = lax.ppermute(grown, axis, [(d, d ^ reach) for d in range(ways)])]
    unnamed x18 -> x17, local copies, waits for them, and re-layouts: 5.61 us -> 3.09 us
  transfers between devices with their start and end apart: 2 -> 7, of which waited for: 1 -> 4; matrix products, arithmetic and copies ran while one was open for 6% -> 30% of each run, Pallas kernels for 0% -> 0%
where the time goes in v1:
time: 242 us; the launch traced here: 241 us
  blocking collectives  77.5 us (32%)
  matrix products  66.4 us (27%)
  waiting for transfers between devices  38.7 us (16%)
  local copies, waits for them, and re-layouts  16.9 us (7%)
  between operations  15 us (6%)
  other arithmetic  13.7 us (6%)
  starting transfers between devices  13.2 us (5%)
    all_gather x1, blocking collectives, body(): lax.all_gather(factors, ('group', 'shard'), axis=0, tiled=True)  46 us
    dot_general x10, matrix products, pool_single(): logits = jnp.dot(sequence, vocab_weight, preferred_element_type=jnp.float32)  43.7 us
    all_to_all x1, waiting for transfers between devices, body(): lax.all_to_all(served, 'shard', split_axis=0, concat_axis=0, tiled=True)  18.5 us
    unnamed x1, blocking collectives  13.1 us
    all_gather x1, waiting for transfers between devices, body(): lax.all_gather(passages, 'shard', axis=0, tiled=True)  13 us
    all_to_all x1, blocking collectives, body(): lax.all_to_all(requests, 'shard', split_axis=0, concat_axis=0, tiled=True)  9.68 us
    all_gather x1, blocking collectives, body(): lax.all_gather(query_coded, 'shard', axis=0, tiled=True)  8.79 us
    ppermute x5, starting transfers between devices, doubled_up(): theirs = lax.ppermute(grown, axis, [(d, d ^ reach) for d in range(ways)])  8.77 us
  transfers between devices with their start and end apart: 7, of which 4 were waited for; matrix products, arithmetic and copies ran while one was open for 30% of the time, Pallas kernels for 0%

profile of v1, /device:TPU:0, one launch (start us, length us, event | category | flops | bytes accessed | tf_op | source)
XLA Modules:
  0.0 241.5 jit_solution(10235218359508459953)
XLA Ops:
  8.6 9.7 %all_to_all.11 = s32[8,1,2]{2,1,0:T(1,128)S(1)} all-to-all(s32[8,1,2]{2,1,0:T(1,128)S(1)} %copy.29), channel_id=1, replica_groups=mesh['group'=4,'shard'=8] {'shard'}, dimensions={0} | all-to-all | bytes 128 | tf_op jit(solution)/shard_map/all_to_all | solution.py:74
  20.4 2.7 %broadcast_select_fusion = bf16[8,2,64,768]{3,2,1,0:T(8,128)(2,1)} fusion(bf16[8,2,64,768]{3,2,1,0:T(8,128)(2,1)} %bitcast.154, pred[8,2]{1,0:T(8,128)(4,1)S(1)} %copy.31), kind=kLoop, calls=%fused_computation.37 | loop fusion | flops 786432 | bytes 3145744 | tf_op jit(solution)/shard_map/jit(_where)/select_n | solution.py:77
  23.1 4.4 %all-to-all-start.1 = ((bf16[8,2,64,768]{3,2,1,0:T(8,128)(2,1)}), bf16[8,2,64,768]{3,2,1,0:T(8,128)(2,1)}, u32[]{:S(2)}, u32[]{:S(2)}) async-start(bf16[8,2,64,768]{3,2,1,0:T(8,128)(2,1)} %broadcast_select_fusion), calls=%async_computation.1 | async-start | bytes 3145728 | tf_op jit(solution)/shard_map/all_to_all | solution.py:78
  30.0 18.5 %all-to-all-done.1 = bf16[8,2,64,768]{3,2,1,0:T(8,128)(2,1)} async-done(((bf16[8,2,64,768]{3,2,1,0:T(8,128)(2,1)}), bf16[8,2,64,768]{3,2,1,0:T(8,128)(2,1)}, u32[]{:S(2)}, u32[]{:S(2)}) %all-to-all-start.1) | async-done | bytes 1572896 | tf_op jit(solution)/shard_map/all_to_all | solution.py:78
  48.6 2.9 %gather_fusion.1 = bf16[8,64,768]{2,1,0:T(8,128)(2,1)} fusion(bf16[16,64,768]{2,1,0:T(8,128)(2,1)} %bitcast.14, s32[1024]{0:T(1024)S(1)} %pad_clamp_fusion), kind=kCustom, calls=%fused_computation.1 | custom fusion | bytes 1572896 | tf_op jit(solution)/shard_map/gather | solution.py:79
  51.4 2.8 %fusion.38 = (u8[64,768]{1,0:T(8,128)(4,1)S(1)}, u8[64,768]{1,0:T(8,128)(4,1)S(1)}, u8[64,768]{1,0:T(8,128)(4,1)S(1)}, f32[8,64,768]{2,1,0:T(8,128)S(1)}) fusion(bf16[8,64,768]{2,1,0:T(8,128)(2,1)} %gather_fusion.1, bf16[768,768]{1,0:T(8,128)(2,1)} %param.15), kind=kOutput, calls=%fused_computation.60 | convolution fusion | flops 611696640 | bytes 3686400 | tf_op jit(solution)/shard_map/dot_general | solution.py:24
  54.3 3.8 %fusion.82 = (f32[8,64]{1,0:T(8,128)S(1)}, f32[8,64,768]{2,1,0:T(8,128)S(1)}) fusion(u8[64,768]{1,0:T(8,128)(4,1)S(1)} %get-tuple-element.38, u8[64,768]{1,0:T(8,128)(4,1)S(1)} %get-tuple-element.39, f32[8,64,768]{2,1,0:T(8,128)S(1)} %get-tuple-element.56, u8[64,768]{1,0:T(8,128)(4,1)S(1)} %get-tuple-element.37), kind=kLoop, calls=%fused_computation.166 | loop fusion | flops 28311040 | bytes 3295232 | tf_op jit(solution)/shard_map/reduce_sum | solution.py:26
  62.0 8.8 %all-gather = bf16[256,768]{1,0:T(8,128)(2,1)S(1)} all-gather(bf16[32,768]{1,0:T(8,128)(2,1)S(1)} %multiply_convert_fusion.2), channel_id=2, replica_groups=mesh['group'=4,'shard'=8] {'shard'}, dimensions={0}, use_global_device_ids=true | all-gather | bytes 442368 | tf_op jit(solution)/shard_map/all_gather | solution.py:61
  77.5 3.0 %collective-permute-done.1 = f32[20,768]{1,0:T(8,128)S(1)} collective-permute-done((f32[20,768]{1,0:T(8,128)S(1)}, f32[20,768]{1,0:T(8,128)S(1)}, u32[]{:S(2)}, u32[]{:S(2)}) %collective-permute-start.1) | collective-permute-done | bytes 61472 | tf_op jit(solution)/shard_map/ppermute | solution.py:15
  89.0 4.1 %collective-permute-done.3 = f32[80,768]{1,0:T(8,128)S(1)} collective-permute-done((f32[80,768]{1,0:T(8,128)S(1)}, f32[80,768]{1,0:T(8,128)S(1)}, u32[]{:S(2)}, u32[]{:S(2)}) %collective-permute-start.3) | collective-permute-done | bytes 245792 | tf_op jit(solution)/shard_map/ppermute | solution.py:15
  96.6 13.0 %all-gather.5.cloned.1.call-done = bf16[1,72,64,768]{3,2,0,1:T(8,128)(2,1)} async-done(((bf16[1,9,64,768]{3,2,0,1:T(8,128)(2,1)}), bf16[1,72,64,768]{3,2,0,1:T(8,128)(2,1)}) %all-gather.5.cloned.1.call-update) | async-done | bytes 7077904 | tf_op jit(solution)/shard_map/all_gather | solution.py:86
  109.6 48.1 %while.2 = (s32[]{:T(128)}, f32[9,8,1920]{2,1,0:T(8,128)}, bf16[9,8,64,768]{3,2,1,0:T(8,128)(2,1)}, bf16[768,1920]{1,0:T(8,128)(2,1)}, s32[]{:T(128)}) while((s32[]{:T(128)}, f32[9,8,1920]{2,1,0:T(8,128)}, bf16[9,8,64,768]{3,2,1,0:T(8,128)(2,1)}, bf16[768,1920]{1,0:T(8,128)(2,1)}, s32[]{:T(128)}) %tuple.40), condition=%wide.region_13.14_spmd, body=%wide.region_11.13_spmd.sunk | while | flops 1511900160 | bytes 3919949 | solution.py:37
  109.6 4.7 %log-plus-one_reduce_fusion.2 = f32[8,1920]{1,0:T(8,128)S(1)} fusion(bf16[768,1920]{1,0:T(8,128)(2,1)} %get-tuple-element.102, bf16[9,8,64,768]{3,2,1,0:T(8,128)(2,1)} %get-tuple-element.101, s32[]{:T(128)S(6)} %copy.45), kind=kOutput, calls=%fused_computation.2.clone.1 | convolution fusion | flops 1511900160 | bytes 3796996 | tf_op jit(solution)/shard_map/while/body/eval_jaxpr/vmap()/dot_general | solution.py:32
  114.9 4.7 %log-plus-one_reduce_fusion.2 = f32[8,1920]{1,0:T(8,128)S(1)} fusion(bf16[768,1920]{1,0:T(8,128)(2,1)} %get-tuple-element.102, bf16[9,8,64,768]{3,2,1,0:T(8,128)(2,1)} %get-tuple-element.101, s32[]{:T(128)S(6)} %copy.45), kind=kOutput, calls=%fused_computation.2.clone.1 | convolution fusion | flops 1511900160 | bytes 3796996 | tf_op jit(solution)/shard_map/while/body/eval_jaxpr/vmap()/dot_general | solution.py:32
  120.3 4.7 %log-plus-one_reduce_fusion.2 = f32[8,1920]{1,0:T(8,128)S(1)} fusion(bf16[768,1920]{1,0:T(8,128)(2,1)} %get-tuple-element.102, bf16[9,8,64,768]{3,2,1,0:T(8,128)(2,1)} %get-tuple-element.101, s32[]{:T(128)S(6)} %copy.45), kind=kOutput, calls=%fused_computation.2.clone.1 | convolution fusion | flops 1511900160 | bytes 3796996 | tf_op jit(solution)/shard_map/while/body/eval_jaxpr/vmap()/dot_general | solution.py:32
  125.6 4.7 %log-plus-one_reduce_fusion.2 = f32[8,1920]{1,0:T(8,128)S(1)} fusion(bf16[768,1920]{1,0:T(8,128)(2,1)} %get-tuple-element.102, bf16[9,8,64,768]{3,2,1,0:T(8,128)(2,1)} %get-tuple-element.101, s32[]{:T(128)S(6)} %copy.45), kind=kOutput, calls=%fused_computation.2.clone.1 | convolution fusion | flops 1511900160 | bytes 3796996 | tf_op jit(solution)/shard_map/while/body/eval_jaxpr/vmap()/dot_general | solution.py:32
  130.9 4.7 %log-plus-one_reduce_fusion.2 = f32[8,1920]{1,0:T(8,128)S(1)} fusion(bf16[768,1920]{1,0:T(8,128)(2,1)} %get-tuple-element.102, bf16[9,8,64,768]{3,2,1,0:T(8,128)(2,1)} %get-tuple-element.101, s32[]{:T(128)S(6)} %copy.45), kind=kOutput, calls=%fused_computation.2.clone.1 | convolution fusion | flops 1511900160 | bytes 3796996 | tf_op jit(solution)/shard_map/while/body/eval_jaxpr/vmap()/dot_general | solution.py:32
  136.3 4.7 %log-plus-one_reduce_fusion.2 = f32[8,1920]{1,0:T(8,128)S(1)} fusion(bf16[768,1920]{1,0:T(8,128)(2,1)} %get-tuple-element.102, bf16[9,8,64,768]{3,2,1,0:T(8,128)(2,1)} %get-tuple-element.101, s32[]{:T(128)S(6)} %copy.45), kind=kOutput, calls=%fused_computation.2.clone.1 | convolution fusion | flops 1511900160 | bytes 3796996 | tf_op jit(solution)/shard_map/while/body/eval_jaxpr/vmap()/dot_general | solution.py:32
  141.6 4.7 %log-plus-one_reduce_fusion.2 = f32[8,1920]{1,0:T(8,128)S(1)} fusion(bf16[768,1920]{1,0:T(8,128)(2,1)} %get-tuple-element.102, bf16[9,8,64,768]{3,2,1,0:T(8,128)(2,1)} %get-tuple-element.101, s32[]{:T(128)S(6)} %copy.45), kind=kOutput, calls=%fused_computation.2.clone.1 | convolution fusion | flops 1511900160 | bytes 3796996 | tf_op jit(solution)/shard_map/while/body/eval_jaxpr/vmap()/dot_general | solution.py:32
  147.0 4.7 %log-plus-one_reduce_fusion.2 = f32[8,1920]{1,0:T(8,128)S(1)} fusion(bf16[768,1920]{1,0:T(8,128)(2,1)} %get-tuple-element.102, bf16[9,8,64,768]{3,2,1,0:T(8,128)(2,1)} %get-tuple-element.101, s32[]{:T(128)S(6)} %copy.45), kind=kOutput, calls=%fused_computation.2.clone.1 | convolution fusion | flops 1511900160 | bytes 3796996 | tf_op jit(solution)/shard_map/while/body/eval_jaxpr/vmap()/dot_general | solution.py:32
  152.3 4.7 %log-plus-one_reduce_fusion.2 = f32[8,1920]{1,0:T(8,128)S(1)} fusion(bf16[768,1920]{1,0:T(8,128)(2,1)} %get-tuple-element.102, bf16[9,8,64,768]{3,2,1,0:T(8,128)(2,1)} %get-tuple-element.101, s32[]{:T(128)S(6)} %copy.45), kind=kOutput, calls=%fused_computation.2.clone.1 | convolution fusion | flops 1511900160 | bytes 3796996 | tf_op jit(solution)/shard_map/while/body/eval_jaxpr/vmap()/dot_general | solution.py:32
  162.2 13.1 %all-reduce = f32[8,9]{1,0:T(8,128)S(1)} all-reduce(f32[8,9]{1,0:T(8,128)S(1)} %bitcast.159), channel_id=4, replica_groups=mesh['group'=4,'shard'=8] {'shard'}, use_global_device_ids=true, to_apply=%region_14.15.clone | all-reduce | flops 72 | bytes 576
  179.1 46.0 %all-gather.2 = f32[32,10,768]{2,1,0:T(8,128)} all-gather(f32[1,10,768]{2,1,0:T(8,128)S(1)} %maximum_bitcast_fusion.1), channel_id=1, replica_groups=mesh['group'=4,'shard'=8] {'group','shard'}, dimensions={0}, use_global_device_ids=true | all-gather | bytes 1013760 | tf_op jit(solution)/shard_map/all_gather | solution.py:125
  227.4 7.2 %fusion.29 = f32[768,768]{1,0:T(8,128)} fusion(f32[320,768]{1,0:T(8,128)} %reshape.544, f32[160,768]{1,0:T(8,128)} %collective-permute-done.4, f32[160,768]{1,0:T(8,128)} %maximum_select_fusion.2, pred[]{:T(512)S(6)} %eq.58), kind=kOutput, calls=%fused_computation.49 | convolution fusion | flops 2265661440 | bytes 4325377 | tf_op jit(solution)/shard_map/rd,re->de/dot_general | solution.py:41
  (96 shorter events, 44.0 us)
Async XLA Ops:
  7.2 11.4 %copy-start = (bf16[32,64,768]{2,1,0:T(8,128)(2,1)S(1)}, bf16[32,64,768]{2,1,0:T(8,128)(2,1)}, u32[]{:S(2)}) copy-start(bf16[32,64,768]{2,1,0:T(8,128)(2,1)} %param.12) | copy-start | bytes 9437188
  23.1 4.5 %copy-start.5 = (s32[1,8]{1,0:T(1,128)S(1)}, s32[1,8]{1,0:T(1,128)}, u32[]{:S(2)}) copy-start(s32[1,8]{1,0:T(1,128)} %param.13) | copy-start | bytes 100
  23.1 4.5 %copy-start.2 = (bf16[1,64,768]{2,1,0:T(8,128)(2,1)S(1)}, bf16[1,64,768]{2,1,0:T(8,128)(2,1)}, u32[]{:S(2)}) copy-start(bf16[1,64,768]{2,1,0:T(8,128)(2,1)} %param.11) | copy-start | bytes 294916
  23.1 25.4 %all-to-all-start.1 = ((bf16[8,2,64,768]{3,2,1,0:T(8,128)(2,1)}), bf16[8,2,64,768]{3,2,1,0:T(8,128)(2,1)}, u32[]{:S(2)}, u32[]{:S(2)}) async-start(bf16[8,2,64,768]{3,2,1,0:T(8,128)(2,1)} %broadcast_select_fusion), calls=%async_computation.1 | async-start | bytes 3145728 | tf_op jit(solution)/shard_map/all_to_all | solution.py:78
  27.6 82.0 %all-gather.5.cloned.1.call-start = ((), (), s32[]{:S(2)}) async-start(), calls=%async_computation.2 | async-start | bytes 7962624 | tf_op jit(solution)/shard_map/all_gather | solution.py:86
  58.7 1.0 copy-start.1
  59.7 12.5 %copy-start.4 = (bf16[768,1920]{1,0:T(8,128)(2,1)S(1)}, bf16[768,1920]{1,0:T(8,128)(2,1)}, u32[]{:S(2)}) copy-start(bf16[768,1920]{1,0:T(8,128)(2,1)} %param.16) | copy-start | bytes 8847364
  71.8 1.9 collective-permute-start
  73.6 10.4 %copy-start.6 = (u32[32]{0:T(128)S(1)}, u32[32]{0:T(128)}, u32[]{:S(2)}) copy-start(u32[32]{0:T(128)} %constant.46) | copy-start | bytes 388
  73.7 6.8 %collective-permute-start.1 = (f32[20,768]{1,0:T(8,128)S(1)}, f32[20,768]{1,0:T(8,128)S(1)}, u32[]{:S(2)}, u32[]{:S(2)}) collective-permute-start(f32[20,768]{1,0:T(8,128)S(1)} %maximum_select_fusion.5), channel_id=1, source_target_pairs={{0,2},{1,3},{2,0},{3,1},{4,6},{5,7},{6,4},{7,5},{8,10},{9,11},{10,... | collective-permute-start | bytes 184328 | tf_op jit(solution)/shard_map/ppermute | solution.py:15
  80.5 5.3 %collective-permute-start.2 = (f32[40,768]{1,0:T(8,128)S(1)}, f32[40,768]{1,0:T(8,128)S(1)}, u32[]{:S(2)}, u32[]{:S(2)}) collective-permute-start(f32[40,768]{1,0:T(8,128)S(1)} %maximum_select_fusion.4), channel_id=1, source_target_pairs={{0,4},{1,5},{2,6},{3,7},{4,0},{5,1},{6,2},{7,3},{8,12},{9,13},{10,... | collective-permute-start | bytes 368648 | tf_op jit(solution)/shard_map/ppermute | solution.py:15
  85.9 7.3 %collective-permute-start.3 = (f32[80,768]{1,0:T(8,128)S(1)}, f32[80,768]{1,0:T(8,128)S(1)}, u32[]{:S(2)}, u32[]{:S(2)}) collective-permute-start(f32[80,768]{1,0:T(8,128)S(1)} %maximum_select_fusion.3), channel_id=1, source_target_pairs={{0,8},{1,9},{2,10},{3,11},{4,12},{5,13},{6,14},{7,15},{8,0},{9,1},... | collective-permute-start | bytes 737288 | tf_op jit(solution)/shard_map/ppermute | solution.py:15
  94.0 133.5 %collective-permute-start.4 = (f32[160,768]{1,0:T(8,128)}, f32[160,768]{1,0:T(8,128)}, u32[]{:S(2)}, u32[]{:S(2)}) collective-permute-start(f32[160,768]{1,0:T(8,128)} %maximum_select_fusion.2), channel_id=1, source_target_pairs={{0,16},{1,17},{2,18},{3,19},{4,20},{5,21},{6,22},{7,23},{8,24},{9,... | collective-permute-start | bytes 1474568 | tf_op jit(solution)/shard_map/ppermute | solution.py:15
  157.7 18.3 %copy-start.3 = (s32[1,8]{1,0:T(1,128)S(1)}, s32[1,8]{1,0:T(1,128)}, u32[]{:S(2)}) copy-start(s32[1,8]{1,0:T(1,128)} %param.14) | copy-start | bytes 100
Sparse Core Ops, SparseCore 0:
  59.8 49.6 all-gather.4
